TPU v7x, 32 devices: a whole 2x2x4 slice. The times are simulated.
32 devices in a mesh: dp: 16 (over z, y, x), mp: 2 (over core).
Axes of the slice: x: 2, y: 2, z: 4, core: 2. Of those that a mesh axis runs over, the one named last changes fastest.
Arguments:
- tokens: bfloat16 [512, 7168], P('dp', 'mp'), may hold values from -6 to 6
- gate_weight: bfloat16 [7168, 18432], P('mp', 'dp'), may hold values from -0.0625 to 0.0625
- up_weight: bfloat16 [7168, 18432], P('mp', 'dp'), may hold values from -0.0625 to 0.0625
- down_weight: bfloat16 [18432, 7168], P('dp', 'mp'), may hold values from -0.046875 to 0.046875
- gate_round: bfloat16 [7168, 18432], P('mp', 'dp'), may hold values from -8 to 8
- up_round: bfloat16 [7168, 18432], P('mp', 'dp'), may hold values from -8 to 8
- down_round: bfloat16 [18432, 7168], P('dp', 'mp'), may hold values from -8 to 8
- quant_scale: float32 [2, 18432], P(None, 'dp'), may hold values from 0.3 to 3
- quant_bits: int32 [2, 18432], P(None, 'dp'), may hold values from 2 to 4
- quant_zero: int32 [2, 18432], P(None, 'dp'), may hold values from 0 to 2
- down_scale: float32 [7168], P('mp'), may hold values from 0.3 to 3
- down_bits: int32 [7168], P('mp'), may hold values from 2 to 4
- down_zero: int32 [7168], P('mp'), may hold values from 0 to 2
- fisher: float32 [512], replicated, may hold values from 1 to 300, as said below
Outputs:
- loss_value: float32 [], replicated
- grad_gate: bfloat16 [7168, 18432], P('mp', 'dp')
- grad_up: bfloat16 [7168, 18432], P('mp', 'dp')
- grad_down: bfloat16 [18432, 7168], P('dp', 'mp')
Inputs may be any that keep to these rules, and one draw needn't show every extreme that they name: `fisher`: positive weights.
All inputs are finite; a program needn't handle non-finite values.
Results may differ from a plain program's by a relative error of at most 0.0059.
Values may be sent and summed in bfloat16 or wider, within the bound.
A program may use at most 192 MiB of HBM per device.

v0:
```python
import jax
import jax.numpy as jnp
from jax import lax
from jax.sharding import PartitionSpec as P

D = 7168
FF = 18432


def soft_weight(weight, variable, channel_scale, bit_width, zero_point, fan_in):
    quant_step = channel_scale / jnp.sqrt(jnp.float32(fan_in))
    offset = jnp.clip(1.2 * jax.nn.sigmoid(variable.astype(jnp.float32)) - 0.1, 0.0, 1.0)
    ceiling = (jnp.left_shift(jnp.int32(1), bit_width) - 1).astype(jnp.float32)
    zero_level = zero_point.astype(jnp.float32)
    levels = jnp.clip(
        weight.astype(jnp.float32) / quant_step + offset - 0.5 + zero_level, 0.0, ceiling
    )
    return (quant_step * (levels - zero_level)).astype(jnp.bfloat16)


def contract_rows(left, right):
    return lax.dot_general(
        left, right, (((0,), (0,)), ((), ())), preferred_element_type=jnp.float32
    )


def shards(
    tokens,
    gate_weight,
    up_weight,
    down_weight,
    gate_round,
    up_round,
    down_round,
    quant_scale,
    quant_bits,
    quant_zero,
    down_scale,
    down_bits,
    down_zero,
    fisher,
):
    own_rows = tokens.shape[0]
    hidden_cols = gate_weight.shape[1]
    all_tokens = lax.all_gather(tokens, "dp", axis=0, tiled=True)
    total_rows = all_tokens.shape[0]
    gate_student = soft_weight(
        gate_weight, gate_round, quant_scale[0], quant_bits[0], quant_zero[0], D
    )
    up_student = soft_weight(up_weight, up_round, quant_scale[1], quant_bits[1], quant_zero[1], D)
    stacked = jnp.concatenate([gate_weight, up_weight, gate_student, up_student], axis=1)
    partial_value = jnp.dot(all_tokens, stacked, preferred_element_type=jnp.float32)
    shares = lax.psum_scatter(partial_value, "mp", scatter_dimension=0, tiled=True)
    gate_teacher = shares[:, :hidden_cols]
    up_teacher = shares[:, hidden_cols : 2 * hidden_cols]
    gate_own = shares[:, 2 * hidden_cols : 3 * hidden_cols]
    up_own = shares[:, 3 * hidden_cols :]
    hidden_teacher = (jax.nn.silu(gate_teacher) * up_teacher).astype(jnp.bfloat16)
    hidden_student = (jax.nn.silu(gate_own) * up_own).astype(jnp.bfloat16)
    hidden = lax.all_gather(
        jnp.concatenate([hidden_teacher, hidden_student], axis=1), "mp", axis=0, tiled=True
    )
    down_student = soft_weight(down_weight, down_round, down_scale, down_bits, down_zero, FF)
    terms = jnp.dot(
        hidden,
        jnp.concatenate([-down_weight, down_student], axis=0),
        preferred_element_type=jnp.float32,
    )
    summed = lax.psum_scatter(terms, "dp", scatter_dimension=0, tiled=True)
    token_weight = lax.dynamic_slice_in_dim(fisher, lax.axis_index("dp") * own_rows, own_rows)
    weighted = token_weight[:, None] * summed
    partial_loss = jnp.sum(weighted * summed)
    local_grad = (2.0 * weighted).astype(jnp.bfloat16)
    loss_sum = lax.psum(partial_loss, ("dp", "mp"))
    out_grad = lax.all_gather(local_grad, "dp", axis=0, tiled=True)
    loss_value = loss_sum / (total_rows * D)
    grad_down = contract_rows(hidden[:, hidden_cols:], out_grad).astype(jnp.bfloat16)
    hidden_part = lax.dot_general(
        out_grad, down_student, (((1,), (1,)), ((), ())), preferred_element_type=jnp.float32
    )
    hidden_grad = lax.psum_scatter(hidden_part, "mp", scatter_dimension=0, tiled=True)
    sigmoid_gate = jax.nn.sigmoid(gate_own)
    gate_grad = (
        hidden_grad * up_own * sigmoid_gate * (1.0 + gate_own * (1.0 - sigmoid_gate))
    ).astype(jnp.bfloat16)
    up_grad = (hidden_grad * gate_own * sigmoid_gate).astype(jnp.bfloat16)
    both_grads = lax.all_gather(
        jnp.concatenate([gate_grad, up_grad], axis=1), "mp", axis=0, tiled=True
    )
    weight_grads = contract_rows(all_tokens, both_grads)
    grad_gate = weight_grads[:, :hidden_cols].astype(jnp.bfloat16)
    grad_up = weight_grads[:, hidden_cols:].astype(jnp.bfloat16)
    return (loss_value, grad_gate, grad_up, grad_down)


def solution(mesh):
    in_specs = (
        P("dp", "mp"),
        P("mp", "dp"),
        P("mp", "dp"),
        P("dp", "mp"),
        P("mp", "dp"),
        P("mp", "dp"),
        P("dp", "mp"),
        P(None, "dp"),
        P(None, "dp"),
        P(None, "dp"),
        P("mp"),
        P("mp"),
        P("mp"),
        P(),
    )
    out_specs = (P(), P("mp", "dp"), P("mp", "dp"), P("dp", "mp"))
    return jax.shard_map(shards, mesh=mesh, in_specs=in_specs, out_specs=out_specs, check_vma=False)
```

profile of v0, /device:TPU:0, one launch (start us, length us, event | category | flops | bytes accessed | tf_op | source)
XLA Modules:
  0.0 532.8 jit_solution(1226961479305919175)
XLA Ops:
  8.8 0.8 convert_reduce_fusion.3
  9.6 0.8 multiply_reduce_fusion.1
  10.4 24.4 %multiply_convert_fusion.1 = (bf16[3584,1152]{1,0:T(8,128)(2,1)}, bf16[3584,1152]{1,0:T(8,128)(2,1)}) fusion(bf16[3584,1152]{1,0:T(8,128)(2,1)} %param.19, bf16[3584,1152]{1,0:T(8,128)(2,1)} %param.16, f32[1152]{0:T(1024)S(1)} %get-tuple-element.13, f32[1152]{0:T(1024)S(1)} %get-tuple-element.11, f32[1152]{0:T(1024)S(1)} %get-tuple-element.9, ...), kind=kLoop, calls=%fused_computation.15 | loop fusion | flops 140378112 | bytes 49572864 | tf_op jit(solution)/shard_map/convert_element_type | solution.py:18
  34.7 50.4 %all-gather.5.cloned.1.call-done = bf16[512,3584]{1,0:T(8,128)(2,1)} async-done(((bf16[32,3584]{1,0:T(8,128)(2,1)}), bf16[512,3584]{1,0:T(8,128)(2,1)}) %all-gather.5.cloned.1.call-update) | async-done | bytes 3670032 | tf_op jit(solution)/shard_map/all_gather | solution.py:45
  85.1 25.0 %fusion.13 = f32[512,4608]{0,1:T(8,128)} fusion(bf16[512,3584]{1,0:T(8,128)(2,1)} %all-gather.5.cloned.1.call-done, bf16[3584,1152]{1,0:T(8,128)(2,1)} %get-tuple-element.22, bf16[3584,1152]{1,0:T(8,128)(2,1)} %get-tuple-element.23, bf16[3584,1152]{1,0:T(8,128)(2,1)} %param.16, bf16[3584,1152]{1,0:T(8,128)(2,1)} %param.15), kind=kOutput, calls=%fused_computation.18 | convolution fusion | flops 17043554304 | bytes 46137344 | tf_op jit(solution)/shard_map/dot_general | solution.py:52
  110.9 15.0 %reduce-scatter.4.cloned.1.call-done = f32[256,4608]{0,1:T(8,128)} async-done(((f32[512,4608]{0,1:T(8,128)}), f32[256,4608]{0,1:T(8,128)}) %reduce-scatter.4.cloned.1.call-update) | async-done | bytes 4718608 | tf_op jit(solution)/shard_map/reduce_scatter | solution.py:53
  125.9 3.0 fusion.17
  128.9 1.1 pad_maximum_fusion
  130.2 14.3 %multiply_convert_fusion = bf16[1152,3584]{1,0:T(8,128)(2,1)} fusion(bf16[1152,3584]{1,0:T(8,128)(2,1)} %param.20, bf16[1152,3584]{1,0:T(8,128)(2,1)} %param.17, f32[3584]{0:T(1024)S(1)} %convert_element_type.84, f32[3584]{0:T(1024)S(1)} %add_convert_fusion, f32[3584]{0:T(1024)S(1)} %broadcast_multiply_fusion), kind=kLoop, calls=%fused_computation.14 | loop fusion | flops 70189056 | bytes 24815616 | tf_op jit(solution)/shard_map/convert_element_type | solution.py:18
  144.5 8.2 %neg.24 = bf16[1152,3584]{1,0:T(8,128)(2,1)} negate(bf16[1152,3584]{1,0:T(8,128)(2,1)} %param.17) | non-fusion elementwise | flops 4128768 | bytes 16515072 | tf_op jit(solution)/shard_map/neg | solution.py:66
  152.7 15.0 %fusion.9 = f32[512,3584]{1,0:T(8,128)} fusion(bf16[512,2304]{0,1:T(8,128)(2,1)} %all-gather.7.cloned.1.call-done, bf16[1152,3584]{1,0:T(8,128)(2,1)} %multiply_convert_fusion, bf16[1152,3584]{1,0:T(8,128)(2,1)} %neg.24), kind=kOutput, calls=%fused_computation.10 | convolution fusion | flops 8488747008 | bytes 26214400 | tf_op jit(solution)/shard_map/dot_general | solution.py:64
  168.5 157.4 %reduce-scatter.6.cloned.1.call-done = f32[32,3584]{1,0:T(8,128)} async-done(((f32[512,3584]{1,0:T(8,128)}), f32[32,3584]{1,0:T(8,128)}) %reduce-scatter.6.cloned.1.call-update) | async-done | bytes 458768 | tf_op jit(solution)/shard_map/reduce_scatter | solution.py:69
  326.0 2.4 fusion.19
  328.5 74.7 %all-gather.9.cloned.1.call-done = bf16[512,3584]{1,0:T(8,128)(2,1)} async-done(((bf16[32,3584]{1,0:T(8,128)(2,1)}), bf16[512,3584]{1,0:T(8,128)(2,1)}) %all-gather.9.cloned.1.call-update) | async-done | bytes 3670032 | tf_op jit(solution)/shard_map/all_gather | solution.py:75
  403.2 10.3 %fusion.23 = f32[512,1152]{0,1:T(8,128)} fusion(bf16[512,3584]{1,0:T(8,128)(2,1)} %all-gather.9.cloned.1.call-done, bf16[1152,3584]{1,0:T(8,128)(2,1)} %multiply_convert_fusion), kind=kOutput, calls=%fused_computation.43 | convolution fusion | flops 4227858432 | bytes 14286848 | tf_op jit(solution)/shard_map/dot_general | solution.py:78
  413.8 8.4 %reduce-scatter.8.cloned.1.call-done = f32[256,1152]{0,1:T(8,128)} async-done(((f32[512,1152]{0,1:T(8,128)}), f32[256,1152]{0,1:T(8,128)}) %reduce-scatter.8.cloned.1.call-update) | async-done | bytes 1179664 | tf_op jit(solution)/shard_map/reduce_scatter | solution.py:81
  422.2 2.5 multiply_convert_fusion.4
  424.7 1.1 pad_maximum_fusion.1
  425.8 40.9 %psum.7 = f32[]{:T(128)} all-reduce(f32[]{:T(128)} %get-tuple-element.21), channel_id=1, replica_groups=mesh['dp'=16,'mp'=2] {'dp','mp'}, use_global_device_ids=true, to_apply=%region_3.4 | all-reduce | flops 1 | bytes 8 | tf_op jit(solution)/shard_map/psum | solution.py:74
  467.3 8.7 %convolution_convert_fusion.1 = bf16[1152,3584]{1,0:T(8,128)(2,1)} fusion(bf16[512,3584]{1,0:T(8,128)(2,1)} %all-gather.9.cloned.1.call-done, bf16[512,2304]{0,1:T(8,128)(2,1)S(1)} %copy-done.3), kind=kOutput, calls=%fused_computation.17 | convolution fusion | flops 4231987200 | bytes 13107200 | tf_op jit(solution)/shard_map/dot_general | solution.py:22
  476.0 14.4 %fusion.8 = bf16[3584,2304]{0,1:T(8,128)(2,1)} fusion(bf16[512,2304]{0,1:T(8,128)(2,1)} %all-gather.11.cloned.1.call-done, bf16[512,3584]{1,0:T(8,128)(2,1)} %all-gather.5.cloned.1.call-done), kind=kOutput, calls=%fused_computation.9 | convolution fusion | flops 8463974400 | bytes 22544384 | tf_op jit(solution)/shard_map/dot_general | solution.py:22
  490.4 11.4 %fusion.22 = (bf16[3584,1152]{0,1:T(8,128)(2,1)}, bf16[3584,1152]{0,1:T(8,128)(2,1)}) fusion(bf16[3584,2304]{0,1:T(8,128)(2,1)} %fusion.8), kind=kLoop, calls=%fused_computation.42 | loop fusion | bytes 33030144 | tf_op jit(solution)/shard_map/slice | solution.py:92
  501.8 11.5 %copy.19 = bf16[3584,1152]{1,0:T(8,128)(2,1)} copy(bf16[3584,1152]{0,1:T(8,128)(2,1)} %get-tuple-element.15) | data formatting | bytes 16515072
  513.3 11.5 %copy.20 = bf16[3584,1152]{1,0:T(8,128)(2,1)} copy(bf16[3584,1152]{0,1:T(8,128)(2,1)} %get-tuple-element.14) | data formatting | bytes 16515072
  (29 shorter events, 3.7 us)
Async XLA Ops:
  7.2 77.9 %all-gather.5.cloned.1.call-start = ((), (), s32[]{:S(2)}) async-start(), calls=%async_computation.3 | async-start | bytes 3899392 | tf_op jit(solution)/shard_map/all_gather | solution.py:45
  7.9 118.0 %reduce-scatter.4.cloned.1.call-start = ((), (), s32[]{:S(2)}) async-start(), calls=%async_computation.4 | async-start | bytes 14155776 | tf_op jit(solution)/shard_map/reduce_scatter | solution.py:53
  110.1 0.7 copy-start
  110.1 0.7 copy-start.1
  110.1 0.7 copy-start.2
  110.1 42.5 %all-gather.7.cloned.1.call-start = ((), (), s32[]{:S(2)}) async-start(), calls=%async_computation.5 | async-start | bytes 3538944 | tf_op jit(solution)/shard_map/all_gather | solution.py:60
  130.0 196.0 %reduce-scatter.6.cloned.1.call-start = ((), (), s32[]{:S(2)}) async-start(), calls=%async_computation.6 | async-start | bytes 7798784 | tf_op jit(solution)/shard_map/reduce_scatter | solution.py:69
  167.7 235.5 %all-gather.9.cloned.1.call-start = ((), (), s32[]{:S(2)}) async-start(), calls=%async_computation.7 | async-start | bytes 3899392 | tf_op jit(solution)/shard_map/all_gather | solution.py:75
  328.4 93.8 %reduce-scatter.8.cloned.1.call-start = ((), (), s32[]{:S(2)}) async-start(), calls=%async_computation.8 | async-start | bytes 3538944 | tf_op jit(solution)/shard_map/reduce_scatter | solution.py:81
  413.5 53.8 %copy-start.3 = (bf16[512,2304]{0,1:T(8,128)(2,1)S(1)}, bf16[512,2304]{0,1:T(8,128)(2,1)}, u32[]{:S(2)}) copy-start(bf16[512,2304]{0,1:T(8,128)(2,1)} %all-gather.7.cloned.1.call-done) | copy-start | bytes 7077892
  413.6 62.5 %all-gather.11.cloned.1.call-start = ((), (), s32[]{:S(2)}) async-start(), calls=%async_computation.9 | async-start | bytes 3538944 | tf_op jit(solution)/shard_map/all_gather | solution.py:87
Sparse Core Ops, SparseCore 0:
  10.7 74.3 all-gather.4
  110.3 15.5 reduce-scatter.3
  130.1 11.7 all-gather.6
  167.8 158.0 reduce-scatter.5
  329.1 73.9 all-gather.8
  413.7 8.4 reduce-scatter.7
  426.0 11.7 all-gather.10
where the time goes:
time: 534 us; the launch traced here: 533 us
  waiting for transfers between devices  307 us (57%)
  matrix products  73.5 us (14%)
  other arithmetic  59.4 us (11%)
  blocking collectives  40.9 us (8%)
  local copies, waits for them, and re-layouts  35.8 us (7%)
  between operations  16 us (3%)
    reduce_scatter x1, waiting for transfers between devices, shards(): summed = lax.psum_scatter(terms, 'dp', scatter_dimension=0, tiled=True)  157 us
    all_gather x1, waiting for transfers between devices, shards(): out_grad = lax.all_gather(local_grad, 'dp', axis=0, tiled=True)  74.7 us
    all_gather x1, waiting for transfers between devices, shards(): all_tokens = lax.all_gather(tokens, 'dp', axis=0, tiled=True)  50.4 us
    psum x1, blocking collectives, shards(): loss_sum = lax.psum(partial_loss, ('dp', 'mp'))  40.9 us
    convert_element_type x2, other arithmetic, soft_weight(): return (quant_step * (levels - zero_level)).astype(jnp.bfloat16)  38.6 us
    dot_general x1, matrix products, shards(): jnp.dot(all_tokens, stacked, preferred_element_type=jnp.float32)  25 us
    unnamed x10, local copies, waits for them, and re-layouts  23.7 us
    dot_general x2, matrix products, contract_rows(): lax.dot_general(left, right, (((0,), (0,)), ((), ())), preferred_element_...  23.1 us
  transfers between devices with their start and end apart: 7, of which 5 were waited for; matrix products, arithmetic and copies ran while one was open for 11% of the time, Pallas kernels for 0%

commit v1 on v0

--- a/solution.py
+++ b/solution.py
@@ -42,7 +42,14 @@
 ):
     own_rows = tokens.shape[0]
     hidden_cols = gate_weight.shape[1]
-    all_tokens = lax.all_gather(tokens, "dp", axis=0, tiled=True)
+    devices = lax.axis_size("dp")
+    hops = [(i, (i + 1) % devices) for i in range(devices)]
+    parts = [tokens]
+    for far in range(1, devices):
+        parts = [lax.ppermute(parts[0], "dp", hops), *parts]
+    whole = jnp.concatenate(parts, axis=0)
+    shift = (lax.axis_index("dp") + 1) * parts[-1].shape[0]
+    all_tokens = jnp.roll(whole, shift, axis=0)
     total_rows = all_tokens.shape[0]
     gate_student = soft_weight(
         gate_weight, gate_round, quant_scale[0], quant_bits[0], quant_zero[0], D

time: 534 us -> 634 us (1.19)
  waiting for transfers between devices: 307 us -> 398 us
  matrix products: 73.5 us -> 81.9 us
    ppermute x0 -> x15, waiting for transfers between devices: none -> 139 us  [shards(): parts = [lax.ppermute(parts[0], 'dp', hops), *parts]]
    all_gather x1 -> x0, waiting for transfers between devices: 50.4 us -> none  [shards(): all_tokens = lax.all_gather(tokens, 'dp', axis=0, tiled=True)]
    dot_general x1, matrix products: 25 us -> 33.4 us  [shards(): jnp.dot(all_tokens, stacked, preferred_element_type=jnp.float32)]
    unnamed x10 -> x67, local copies, waits for them, and re-layouts: 23.7 us -> 18.4 us
  transfers between devices with their start and end apart: 7 -> 21, of which waited for: 5 -> 18; matrix products, arithmetic and copies ran while one was open for 11% -> 9% of each run, Pallas kernels for 0% -> 0%
where the time goes in v1:
time: 634 us; the launch traced here: 633 us
  waiting for transfers between devices  398 us (63%)
  matrix products  81.9 us (13%)
  other arithmetic  59.3 us (9%)
  blocking collectives  41.1 us (6%)
  local copies, waits for them, and re-layouts  32.8 us (5%)
  between operations  16.3 us (3%)
    reduce_scatter x1, waiting for transfers between devices, shards(): summed = lax.psum_scatter(terms, 'dp', scatter_dimension=0, tiled=True)  157 us
    ppermute x15, waiting for transfers between devices, shards(): parts = [lax.ppermute(parts[0], 'dp', hops), *parts]  139 us
    all_gather x1, waiting for transfers between devices, shards(): out_grad = lax.all_gather(local_grad, 'dp', axis=0, tiled=True)  74.7 us
    psum x1, blocking collectives, shards(): loss_sum = lax.psum(partial_loss, ('dp', 'mp'))  41.1 us
    convert_element_type x2, other arithmetic, soft_weight(): return (quant_step * (levels - zero_level)).astype(jnp.bfloat16)  38.4 us
    dot_general x1, matrix products, shards(): jnp.dot(all_tokens, stacked, preferred_element_type=jnp.float32)  33.4 us
    dot_general x2, matrix products, contract_rows(): lax.dot_general(left, right, (((0,), (0,)), ((), ())), preferred_element_...  22.9 us
    unnamed x67, local copies, waits for them, and re-layouts  18.4 us
  transfers between devices with their start and end apart: 21, of which 18 were waited for; matrix products, arithmetic and copies ran while one was open for 9% of the time, Pallas kernels for 0%

profile of v1, /device:TPU:0, one launch (start us, length us, event | category | flops | bytes accessed | tf_op | source)
XLA Modules:
  0.0 632.8 jit_solution(673930618076973902)
XLA Ops:
  10.2 9.8 %collective-permute-done = bf16[32,3584]{1,0:T(8,128)(2,1)S(1)} collective-permute-done((bf16[32,3584]{1,0:T(8,128)(2,1)}, bf16[32,3584]{1,0:T(8,128)(2,1)S(1)}, u32[]{:S(2)}, u32[]{:S(2)}) %collective-permute-start) | collective-permute-done | bytes 229408 | tf_op jit(solution)/shard_map/ppermute | solution.py:49
  20.0 10.4 %collective-permute-done.1 = bf16[32,3584]{1,0:T(8,128)(2,1)S(1)} collective-permute-done((bf16[32,3584]{1,0:T(8,128)(2,1)S(1)}, bf16[32,3584]{1,0:T(8,128)(2,1)S(1)}, u32[]{:S(2)}, u32[]{:S(2)}) %collective-permute-start.1) | collective-permute-done | bytes 229408 | tf_op jit(solution)/shard_map/ppermute | solution.py:49
  30.4 9.6 %collective-permute-done.2 = bf16[32,3584]{1,0:T(8,128)(2,1)S(1)} collective-permute-done((bf16[32,3584]{1,0:T(8,128)(2,1)S(1)}, bf16[32,3584]{1,0:T(8,128)(2,1)S(1)}, u32[]{:S(2)}, u32[]{:S(2)}) %collective-permute-start.2) | collective-permute-done | bytes 229408 | tf_op jit(solution)/shard_map/ppermute | solution.py:49
  40.0 9.6 %collective-permute-done.3 = bf16[32,3584]{1,0:T(8,128)(2,1)S(1)} collective-permute-done((bf16[32,3584]{1,0:T(8,128)(2,1)S(1)}, bf16[32,3584]{1,0:T(8,128)(2,1)S(1)}, u32[]{:S(2)}, u32[]{:S(2)}) %collective-permute-start.3) | collective-permute-done | bytes 229408 | tf_op jit(solution)/shard_map/ppermute | solution.py:49
  49.6 9.6 %collective-permute-done.4 = bf16[32,3584]{1,0:T(8,128)(2,1)S(1)} collective-permute-done((bf16[32,3584]{1,0:T(8,128)(2,1)S(1)}, bf16[32,3584]{1,0:T(8,128)(2,1)S(1)}, u32[]{:S(2)}, u32[]{:S(2)}) %collective-permute-start.4) | collective-permute-done | bytes 229408 | tf_op jit(solution)/shard_map/ppermute | solution.py:49
  59.3 9.6 %collective-permute-done.5 = bf16[32,3584]{1,0:T(8,128)(2,1)S(1)} collective-permute-done((bf16[32,3584]{1,0:T(8,128)(2,1)S(1)}, bf16[32,3584]{1,0:T(8,128)(2,1)S(1)}, u32[]{:S(2)}, u32[]{:S(2)}) %collective-permute-start.5) | collective-permute-done | bytes 229408 | tf_op jit(solution)/shard_map/ppermute | solution.py:49
  68.9 10.8 %collective-permute-done.6 = bf16[32,3584]{1,0:T(8,128)(2,1)S(1)} collective-permute-done((bf16[32,3584]{1,0:T(8,128)(2,1)S(1)}, bf16[32,3584]{1,0:T(8,128)(2,1)S(1)}, u32[]{:S(2)}, u32[]{:S(2)}) %collective-permute-start.6) | collective-permute-done | bytes 229408 | tf_op jit(solution)/shard_map/ppermute | solution.py:49
  79.6 11.9 %collective-permute-done.7 = bf16[32,3584]{1,0:T(8,128)(2,1)S(1)} collective-permute-done((bf16[32,3584]{1,0:T(8,128)(2,1)S(1)}, bf16[32,3584]{1,0:T(8,128)(2,1)S(1)}, u32[]{:S(2)}, u32[]{:S(2)}) %collective-permute-start.7) | collective-permute-done | bytes 229408 | tf_op jit(solution)/shard_map/ppermute | solution.py:49
  91.6 11.2 %collective-permute-done.8 = bf16[32,3584]{1,0:T(8,128)(2,1)S(1)} collective-permute-done((bf16[32,3584]{1,0:T(8,128)(2,1)S(1)}, bf16[32,3584]{1,0:T(8,128)(2,1)S(1)}, u32[]{:S(2)}, u32[]{:S(2)}) %collective-permute-start.8) | collective-permute-done | bytes 229408 | tf_op jit(solution)/shard_map/ppermute | solution.py:49
  102.8 10.4 %collective-permute-done.9 = bf16[32,3584]{1,0:T(8,128)(2,1)S(1)} collective-permute-done((bf16[32,3584]{1,0:T(8,128)(2,1)S(1)}, bf16[32,3584]{1,0:T(8,128)(2,1)S(1)}, u32[]{:S(2)}, u32[]{:S(2)}) %collective-permute-start.9) | collective-permute-done | bytes 229408 | tf_op jit(solution)/shard_map/ppermute | solution.py:49
  113.1 9.6 %collective-permute-done.10 = bf16[32,3584]{1,0:T(8,128)(2,1)S(1)} collective-permute-done((bf16[32,3584]{1,0:T(8,128)(2,1)S(1)}, bf16[32,3584]{1,0:T(8,128)(2,1)S(1)}, u32[]{:S(2)}, u32[]{:S(2)}) %collective-permute-start.10) | collective-permute-done | bytes 229408 | tf_op jit(solution)/shard_map/ppermute | solution.py:49
  122.8 9.6 %collective-permute-done.11 = bf16[32,3584]{1,0:T(8,128)(2,1)S(1)} collective-permute-done((bf16[32,3584]{1,0:T(8,128)(2,1)S(1)}, bf16[32,3584]{1,0:T(8,128)(2,1)S(1)}, u32[]{:S(2)}, u32[]{:S(2)}) %collective-permute-start.11) | collective-permute-done | bytes 229408 | tf_op jit(solution)/shard_map/ppermute | solution.py:49
  132.4 9.6 %collective-permute-done.12 = bf16[32,3584]{1,0:T(8,128)(2,1)S(1)} collective-permute-done((bf16[32,3584]{1,0:T(8,128)(2,1)S(1)}, bf16[32,3584]{1,0:T(8,128)(2,1)S(1)}, u32[]{:S(2)}, u32[]{:S(2)}) %collective-permute-start.12) | collective-permute-done | bytes 229408 | tf_op jit(solution)/shard_map/ppermute | solution.py:49
  151.7 24.2 %multiply_convert_fusion.1 = (bf16[3584,1152]{1,0:T(8,128)(2,1)}, bf16[3584,1152]{1,0:T(8,128)(2,1)}) fusion(bf16[3584,1152]{1,0:T(8,128)(2,1)} %param.19, bf16[3584,1152]{1,0:T(8,128)(2,1)} %param.16, f32[1152]{0:T(1024)S(1)} %get-tuple-element.9, f32[1152]{0:T(1024)S(1)} %get-tuple-element.7, f32[1152]{0:T(1024)S(1)} %get-tuple-element.5, ...), kind=kLoop, calls=%fused_computation.14 | loop fusion | flops 140378112 | bytes 49572864 | tf_op jit(solution)/shard_map/convert_element_type | solution.py:18
  196.3 33.4 %fusion = f32[512,4608]{1,0:T(8,128)} fusion(bf16[3584,1152]{1,0:T(8,128)(2,1)} %get-tuple-element.18, bf16[3584,1152]{1,0:T(8,128)(2,1)} %get-tuple-element.19, bf16[3584,1152]{1,0:T(8,128)(2,1)S(1)} %bitcast.7, bf16[3584,1152]{1,0:T(8,128)(2,1)S(1)} %copy-done, bf16[512,3584]{1,0:T(8,128)(2,1)} %fusion.35), kind=kOutput, calls=%fused_computation | convolution fusion | flops 17043554304 | bytes 46137344 | tf_op jit(solution)/shard_map/dot_general | solution.py:59
  230.4 18.0 %reduce-scatter.4.cloned.1.call-done = f32[256,4608]{1,0:T(8,128)} async-done(((f32[512,4608]{1,0:T(8,128)}), f32[256,4608]{1,0:T(8,128)}) %reduce-scatter.4.cloned.1.call-update) | async-done | bytes 4718608 | tf_op jit(solution)/shard_map/reduce_scatter | solution.py:60
  252.7 14.2 %multiply_convert_fusion = bf16[1152,3584]{1,0:T(8,128)(2,1)} fusion(bf16[1152,3584]{1,0:T(8,128)(2,1)} %param.20, bf16[1152,3584]{1,0:T(8,128)(2,1)} %param.17, f32[3584]{0:T(1024)S(1)} %convert_element_type.84, f32[3584]{0:T(1024)S(1)} %add_convert_fusion, f32[3584]{0:T(1024)S(1)} %broadcast_multiply_fusion), kind=kLoop, calls=%fused_computation.13 | loop fusion | flops 70189056 | bytes 24815616 | tf_op jit(solution)/shard_map/convert_element_type | solution.py:18
  275.1 14.8 %fusion.8 = f32[512,3584]{1,0:T(8,128)} fusion(bf16[512,2304]{1,0:T(8,128)(2,1)} %all-gather.4.cloned.1.call-done, bf16[1152,3584]{1,0:T(8,128)(2,1)} %multiply_convert_fusion, bf16[1152,3584]{1,0:T(8,128)(2,1)} %neg.24), kind=kOutput, calls=%fused_computation.9 | convolution fusion | flops 8488747008 | bytes 26214400 | tf_op jit(solution)/shard_map/dot_general | solution.py:71
  290.7 157.4 %reduce-scatter.6.cloned.1.call-done = f32[32,3584]{1,0:T(8,128)} async-done(((f32[512,3584]{1,0:T(8,128)}), f32[32,3584]{1,0:T(8,128)}) %reduce-scatter.6.cloned.1.call-update) | async-done | bytes 458768 | tf_op jit(solution)/shard_map/reduce_scatter | solution.py:76
  450.7 74.7 %all-gather.6.cloned.1.call-done = bf16[512,3584]{1,0:T(8,128)(2,1)} async-done(((bf16[32,3584]{1,0:T(8,128)(2,1)}), bf16[512,3584]{1,0:T(8,128)(2,1)}) %all-gather.6.cloned.1.call-update) | async-done | bytes 3670032 | tf_op jit(solution)/shard_map/all_gather | solution.py:82
  525.4 10.8 %fusion.23 = f32[512,1152]{1,0:T(8,128)} fusion(bf16[512,3584]{1,0:T(8,128)(2,1)} %all-gather.6.cloned.1.call-done, bf16[1152,3584]{1,0:T(8,128)(2,1)} %multiply_convert_fusion), kind=kOutput, calls=%fused_computation.77 | convolution fusion | flops 4227858432 | bytes 14286848 | tf_op jit(solution)/shard_map/dot_general | solution.py:85
  548.6 41.1 %psum.7 = f32[]{:T(128)} all-reduce(f32[]{:T(128)} %get-tuple-element.17), channel_id=1, replica_groups=mesh['dp'=16,'mp'=2] {'dp','mp'}, use_global_device_ids=true, to_apply=%region_3.4 | all-reduce | flops 1 | bytes 8 | tf_op jit(solution)/shard_map/psum | solution.py:81
  598.9 14.4 %convolution_convert_fusion = bf16[3584,2304]{1,0:T(8,128)(2,1)} fusion(bf16[512,2304]{1,0:T(8,128)(2,1)} %all-gather.8.cloned.1.call-done, bf16[1024,3584]{1,0:T(8,128)(2,1)} %copy-done.1, s32[]{:T(128)S(6)} %select_n.18), kind=kOutput, calls=%fused_computation.8 | convolution fusion | flops 8463974400 | bytes 22544388 | tf_op jit(solution)/shard_map/dot_general | solution.py:22
  613.3 11.5 %fusion.22 = (bf16[3584,1152]{1,0:T(8,128)(2,1)}, bf16[3584,1152]{1,0:T(8,128)(2,1)}) fusion(bf16[3584,2304]{1,0:T(8,128)(2,1)} %convolution_convert_fusion), kind=kLoop, calls=%fused_computation.76 | loop fusion | bytes 33030144 | tf_op jit(solution)/shard_map/slice | solution.py:99
  (116 shorter events, 70.2 us)
Async XLA Ops:
  7.2 241.3 %reduce-scatter.4.cloned.1.call-start = ((), (), s32[]{:S(2)}) async-start(), calls=%async_computation.3 | async-start | bytes 14155776 | tf_op jit(solution)/shard_map/reduce_scatter | solution.py:60
  7.2 12.8 %collective-permute-start = (bf16[32,3584]{1,0:T(8,128)(2,1)}, bf16[32,3584]{1,0:T(8,128)(2,1)S(1)}, u32[]{:S(2)}, u32[]{:S(2)}) collective-permute-start(bf16[32,3584]{1,0:T(8,128)(2,1)} %param.14), channel_id=1, source_target_pairs={{0,2},{2,4},{4,6},{6,8},{8,10},{10,12},{12,14},{14,16},{16,18},{18... | collective-permute-start | bytes 688136 | tf_op jit(solution)/shard_map/ppermute | solution.py:49
  20.0 10.4 %collective-permute-start.1 = (bf16[32,3584]{1,0:T(8,128)(2,1)S(1)}, bf16[32,3584]{1,0:T(8,128)(2,1)S(1)}, u32[]{:S(2)}, u32[]{:S(2)}) collective-permute-start(bf16[32,3584]{1,0:T(8,128)(2,1)S(1)} %collective-permute-done), channel_id=1, source_target_pairs={{0,2},{2,4},{4,6},{6,8},{8,10},{10,12},{12,14},{14,16},{16,18},{18... | collective-permute-start | bytes 688136 | tf_op jit(solution)/shard_map/ppermute | solution.py:49
  30.4 9.6 %collective-permute-start.2 = (bf16[32,3584]{1,0:T(8,128)(2,1)S(1)}, bf16[32,3584]{1,0:T(8,128)(2,1)S(1)}, u32[]{:S(2)}, u32[]{:S(2)}) collective-permute-start(bf16[32,3584]{1,0:T(8,128)(2,1)S(1)} %collective-permute-done.1), channel_id=1, source_target_pairs={{0,2},{2,4},{4,6},{6,8},{8,10},{10,12},{12,14},{14,16},{16,18},{18... | collective-permute-start | bytes 688136 | tf_op jit(solution)/shard_map/ppermute | solution.py:49
  40.0 9.6 %collective-permute-start.3 = (bf16[32,3584]{1,0:T(8,128)(2,1)S(1)}, bf16[32,3584]{1,0:T(8,128)(2,1)S(1)}, u32[]{:S(2)}, u32[]{:S(2)}) collective-permute-start(bf16[32,3584]{1,0:T(8,128)(2,1)S(1)} %collective-permute-done.2), channel_id=1, source_target_pairs={{0,2},{2,4},{4,6},{6,8},{8,10},{10,12},{12,14},{14,16},{16,18},{18... | collective-permute-start | bytes 688136 | tf_op jit(solution)/shard_map/ppermute | solution.py:49
  49.6 9.6 %collective-permute-start.4 = (bf16[32,3584]{1,0:T(8,128)(2,1)S(1)}, bf16[32,3584]{1,0:T(8,128)(2,1)S(1)}, u32[]{:S(2)}, u32[]{:S(2)}) collective-permute-start(bf16[32,3584]{1,0:T(8,128)(2,1)S(1)} %collective-permute-done.3), channel_id=1, source_target_pairs={{0,2},{2,4},{4,6},{6,8},{8,10},{10,12},{12,14},{14,16},{16,18},{18... | collective-permute-start | bytes 688136 | tf_op jit(solution)/shard_map/ppermute | solution.py:49
  59.3 118.9 %copy-start.3 = (bf16[32,3584]{1,0:T(8,128)(2,1)}, bf16[32,3584]{1,0:T(8,128)(2,1)S(1)}, u32[]{:S(2)}) copy-start(bf16[32,3584]{1,0:T(8,128)(2,1)S(1)} %collective-permute-done.4) | copy-start | bytes 688132
  59.3 9.6 %collective-permute-start.5 = (bf16[32,3584]{1,0:T(8,128)(2,1)S(1)}, bf16[32,3584]{1,0:T(8,128)(2,1)S(1)}, u32[]{:S(2)}, u32[]{:S(2)}) collective-permute-start(bf16[32,3584]{1,0:T(8,128)(2,1)S(1)} %collective-permute-done.4), channel_id=1, source_target_pairs={{0,2},{2,4},{4,6},{6,8},{8,10},{10,12},{12,14},{14,16},{16,18},{18... | collective-permute-start | bytes 688136 | tf_op jit(solution)/shard_map/ppermute | solution.py:49
  68.9 109.3 %copy-start.4 = (bf16[32,3584]{1,0:T(8,128)(2,1)}, bf16[32,3584]{1,0:T(8,128)(2,1)S(1)}, u32[]{:S(2)}) copy-start(bf16[32,3584]{1,0:T(8,128)(2,1)S(1)} %collective-permute-done.5) | copy-start | bytes 688132
  68.9 10.8 %collective-permute-start.6 = (bf16[32,3584]{1,0:T(8,128)(2,1)S(1)}, bf16[32,3584]{1,0:T(8,128)(2,1)S(1)}, u32[]{:S(2)}, u32[]{:S(2)}) collective-permute-start(bf16[32,3584]{1,0:T(8,128)(2,1)S(1)} %collective-permute-done.5), channel_id=1, source_target_pairs={{0,2},{2,4},{4,6},{6,8},{8,10},{10,12},{12,14},{14,16},{16,18},{18... | collective-permute-start | bytes 688136 | tf_op jit(solution)/shard_map/ppermute | solution.py:49
  79.6 98.5 %copy-start.5 = (bf16[32,3584]{1,0:T(8,128)(2,1)}, bf16[32,3584]{1,0:T(8,128)(2,1)S(1)}, u32[]{:S(2)}) copy-start(bf16[32,3584]{1,0:T(8,128)(2,1)S(1)} %collective-permute-done.6) | copy-start | bytes 688132
  79.6 11.9 %collective-permute-start.7 = (bf16[32,3584]{1,0:T(8,128)(2,1)S(1)}, bf16[32,3584]{1,0:T(8,128)(2,1)S(1)}, u32[]{:S(2)}, u32[]{:S(2)}) collective-permute-start(bf16[32,3584]{1,0:T(8,128)(2,1)S(1)} %collective-permute-done.6), channel_id=1, source_target_pairs={{0,2},{2,4},{4,6},{6,8},{8,10},{10,12},{12,14},{14,16},{16,18},{18... | collective-permute-start | bytes 688136 | tf_op jit(solution)/shard_map/ppermute | solution.py:49
  91.6 11.2 %collective-permute-start.8 = (bf16[32,3584]{1,0:T(8,128)(2,1)S(1)}, bf16[32,3584]{1,0:T(8,128)(2,1)S(1)}, u32[]{:S(2)}, u32[]{:S(2)}) collective-permute-start(bf16[32,3584]{1,0:T(8,128)(2,1)S(1)} %collective-permute-done.7), channel_id=1, source_target_pairs={{0,2},{2,4},{4,6},{6,8},{8,10},{10,12},{12,14},{14,16},{16,18},{18... | collective-permute-start | bytes 688136 | tf_op jit(solution)/shard_map/ppermute | solution.py:49
  102.8 10.4 %collective-permute-start.9 = (bf16[32,3584]{1,0:T(8,128)(2,1)S(1)}, bf16[32,3584]{1,0:T(8,128)(2,1)S(1)}, u32[]{:S(2)}, u32[]{:S(2)}) collective-permute-start(bf16[32,3584]{1,0:T(8,128)(2,1)S(1)} %collective-permute-done.8), channel_id=1, source_target_pairs={{0,2},{2,4},{4,6},{6,8},{8,10},{10,12},{12,14},{14,16},{16,18},{18... | collective-permute-start | bytes 688136 | tf_op jit(solution)/shard_map/ppermute | solution.py:49
  113.1 9.6 %collective-permute-start.10 = (bf16[32,3584]{1,0:T(8,128)(2,1)S(1)}, bf16[32,3584]{1,0:T(8,128)(2,1)S(1)}, u32[]{:S(2)}, u32[]{:S(2)}) collective-permute-start(bf16[32,3584]{1,0:T(8,128)(2,1)S(1)} %collective-permute-done.9), channel_id=1, source_target_pairs={{0,2},{2,4},{4,6},{6,8},{8,10},{10,12},{12,14},{14,16},{16,18},{18... | collective-permute-start | bytes 688136 | tf_op jit(solution)/shard_map/ppermute | solution.py:49
  122.8 9.6 %collective-permute-start.11 = (bf16[32,3584]{1,0:T(8,128)(2,1)S(1)}, bf16[32,3584]{1,0:T(8,128)(2,1)S(1)}, u32[]{:S(2)}, u32[]{:S(2)}) collective-permute-start(bf16[32,3584]{1,0:T(8,128)(2,1)S(1)} %collective-permute-done.10), channel_id=1, source_target_pairs={{0,2},{2,4},{4,6},{6,8},{8,10},{10,12},{12,14},{14,16},{16,18},{18... | collective-permute-start | bytes 688136 | tf_op jit(solution)/shard_map/ppermute | solution.py:49
  132.4 9.6 %collective-permute-start.12 = (bf16[32,3584]{1,0:T(8,128)(2,1)S(1)}, bf16[32,3584]{1,0:T(8,128)(2,1)S(1)}, u32[]{:S(2)}, u32[]{:S(2)}) collective-permute-start(bf16[32,3584]{1,0:T(8,128)(2,1)S(1)} %collective-permute-done.11), channel_id=1, source_target_pairs={{0,2},{2,4},{4,6},{6,8},{8,10},{10,12},{12,14},{14,16},{16,18},{18... | collective-permute-start | bytes 688136 | tf_op jit(solution)/shard_map/ppermute | solution.py:49
  142.0 9.7 %collective-permute-start.13 = (bf16[32,3584]{1,0:T(8,128)(2,1)S(1)}, bf16[32,3584]{1,0:T(8,128)(2,1)}, u32[]{:S(2)}, u32[]{:S(2)}) collective-permute-start(bf16[32,3584]{1,0:T(8,128)(2,1)S(1)} %collective-permute-done.12), channel_id=1, source_target_pairs={{0,2},{2,4},{4,6},{6,8},{8,10},{10,12},{12,14},{14,16},{16,18},{18... | collective-permute-start | bytes 688136 | tf_op jit(solution)/shard_map/ppermute | solution.py:49
  151.7 24.3 %collective-permute-start.14 = (bf16[32,3584]{1,0:T(8,128)(2,1)}, bf16[32,3584]{1,0:T(8,128)(2,1)}, u32[]{:S(2)}, u32[]{:S(2)}) collective-permute-start(bf16[32,3584]{1,0:T(8,128)(2,1)} %collective-permute-done.13), channel_id=1, source_target_pairs={{0,2},{2,4},{4,6},{6,8},{8,10},{10,12},{12,14},{14,16},{16,18},{18... | collective-permute-start | bytes 688136 | tf_op jit(solution)/shard_map/ppermute | solution.py:49
  229.7 45.3 %all-gather.4.cloned.1.call-start = ((), (), s32[]{:S(2)}) async-start(), calls=%async_computation.4 | async-start | bytes 3538944 | tf_op jit(solution)/shard_map/all_gather | solution.py:67
  252.6 195.5 %reduce-scatter.6.cloned.1.call-start = ((), (), s32[]{:S(2)}) async-start(), calls=%async_computation.5 | async-start | bytes 7798784 | tf_op jit(solution)/shard_map/reduce_scatter | solution.py:76
  289.9 235.5 %all-gather.6.cloned.1.call-start = ((), (), s32[]{:S(2)}) async-start(), calls=%async_computation.6 | async-start | bytes 3899392 | tf_op jit(solution)/shard_map/all_gather | solution.py:82
  450.6 94.4 %reduce-scatter.8.cloned.1.call-start = ((), (), s32[]{:S(2)}) async-start(), calls=%async_computation.7 | async-start | bytes 3538944 | tf_op jit(solution)/shard_map/reduce_scatter | solution.py:88
  536.2 62.7 %all-gather.8.cloned.1.call-start = ((), (), s32[]{:S(2)}) async-start(), calls=%async_computation.8 | async-start | bytes 3538944 | tf_op jit(solution)/shard_map/all_gather | solution.py:94
  (15 other events, 491.9 us)
Sparse Core Ops, SparseCore 0:
  229.8 18.5 reduce-scatter.3
  252.7 12.2 all-gather.3
  290.0 158.0 reduce-scatter.5
  451.3 73.9 all-gather.5
  536.3 8.6 reduce-scatter.7
  548.8 12.2 all-gather.7
